TPU v7x, 512 devices: a whole 4x4x16 slice. The times are simulated.
512 devices in a mesh: gx: 32 (over y, x, core), gy: 16 (over z).
Axes of the slice: x: 4, y: 4, z: 16, core: 2. Of those that a mesh axis runs over, the one named last changes fastest.
Arguments:
- start: float32 [64, 16, 1024], P('gx', 'gy'), may hold values from -6 to 6
- source: float32 [64, 16, 1024], P('gx', 'gy'), may hold values from -4 to 4
- diag_inverse: bfloat16 [64, 16, 16, 4096], P('gx', 'gy'), may hold values from -0.75 to 0.75
- x_lower: bfloat16 [64, 16, 16, 4096], P('gx', 'gy'), may hold values from -1 to 1
- x_upper: bfloat16 [64, 16, 16, 4096], P('gx', 'gy'), may hold values from -1 to 1
- side_blocks: bfloat16 [4, 64, 16, 16, 4096], P(None, 'gx', 'gy'), may hold values from -0.25 to 0.25
Outputs:
- forward: float32 [64, 16, 1024], P('gx', 'gy')
- result: float32 [64, 16, 1024], P('gx', 'gy')
All inputs are finite; a program needn't handle non-finite values.
Results may differ from a plain program's by a relative error of at most 0.0003.
Values sent between devices are 32-bit elements; how exact they have to be, the bound alone decides.
A program may use at most 64 MiB of HBM per device.

v0:
```python
import jax
import jax.numpy as jnp
from jax import lax
from jax.sharding import PartitionSpec as P


def padded(block, sides, width):
    for axis, dim in sides:
        count = lax.axis_size(axis)
        forward = [(i, i + 1) for i in range(count - 1)]
        backward = [(target, source) for source, target in forward]
        low = lax.ppermute(
            lax.slice_in_dim(block, block.shape[dim] - width, None, axis=dim), axis, forward
        )
        high = lax.ppermute(lax.slice_in_dim(block, 0, width, axis=dim), axis, backward)
        block = jnp.concatenate([low, block, high], axis=dim)
    return block


def from_behind(block, axis, distance):
    devices = range(lax.axis_size(axis))
    route = [(i - distance, i) for i in devices if i - distance in devices]
    return lax.ppermute(block, axis, route)


def prefix_2(part, axis, combine, identity, reverse):
    count = lax.axis_size(axis)
    place = lax.axis_index(axis)
    ahead = count - 1 - place if reverse else place
    gathered = jax.tree.map(lambda a: lax.all_gather(a, axis), part)
    state = jax.tree.map(lambda a, e: jnp.zeros_like(a) + jnp.asarray(e, a.dtype), part, identity)

    def one(hop, state):
        source = count - 1 - hop if reverse else hop
        return combine(
            state, jax.tree.map(lambda a: lax.dynamic_index_in_dim(a, source, 0, False), gathered)
        )

    return lax.fori_loop(0, ahead, one, state)


def apply_block(block, column_values):
    lead = column_values.shape[:-1]
    depth = block.shape[-2]
    width = column_values.shape[-1] // depth
    matrix = block.astype(jnp.float32).reshape(lead + (depth, width, width))
    column = column_values.reshape(lead + (depth, width))
    product = jnp.einsum("...zab,...zb->...za", matrix, column, precision=lax.Precision.HIGHEST)
    return product.reshape(lead + (depth * width,))


def z_terms(side_blocks, column_values, depth):
    width = column_values.shape[-1] // depth
    cells = column_values.reshape(column_values.shape[:-1] + (depth, width))
    zero = jnp.zeros_like(cells[..., :1, :])
    below = jnp.concatenate([zero, cells[..., :-1, :]], -2).reshape(column_values.shape)
    above = jnp.concatenate([cells[..., 1:, :], zero], -2).reshape(column_values.shape)
    return apply_block(side_blocks[2], below) + apply_block(side_blocks[3], above)


def multiply_maps(later, earlier, depth):
    rows = later.shape[0]
    width = later.shape[-1]
    species = int(width**0.5 + 0.5)
    left = later.astype(jnp.float32).reshape(rows, depth, species, species)
    right = earlier.astype(jnp.float32).reshape(rows, depth, species, species)
    joined = jnp.einsum("yzab,yzbc->yzac", left, right, precision=lax.Precision.HIGHEST)
    return joined.reshape(rows, depth, width)


def compose_planes(drive, blocks, depth, order):
    first = order[0]
    product = blocks[first].astype(jnp.float32)
    offset = drive[first]
    for plane in order[1:]:
        offset = drive[plane] - apply_block(blocks[plane], offset)
        product = multiply_maps(blocks[plane], product, depth)
    return (product, offset)


def run_planes(drive, blocks, entering, order):
    planes = [None] * drive.shape[0]
    previous = entering
    for plane in order:
        previous = drive[plane] - apply_block(blocks[plane], previous)
        planes[plane] = previous
    return jnp.stack(planes, 0)


def make_combine(depth):

    def combine(earlier, later):
        matrix = multiply_maps(later[0], earlier[0], depth)
        offset = later[1] + apply_block(later[0], earlier[1])
        return (matrix, offset)

    return combine


def neutral_map(rows, depth, species):
    unit_matrix = jnp.eye(species, dtype=jnp.float32).reshape(1, 1, species * species)
    matrix = jnp.broadcast_to(unit_matrix, (rows, depth, species * species))
    return (matrix, jnp.zeros((rows, depth * species), jnp.float32))


def local(start, source, diag_inverse, x_lower, x_upper, side_blocks):
    depth = x_lower.shape[2]
    rows = start.shape[1]
    planes_here = start.shape[0]
    species = start.shape[2] // depth
    upward = list(range(planes_here))
    downward = upward[::-1]
    combine = make_combine(depth)
    rhs = apply_block(diag_inverse, source)
    sideways = padded(start, (("gy", 1),), 1)
    ahead_plane = from_behind(start[:1], "gx", -1)
    ahead = jnp.concatenate([start[1:], ahead_plane], 0)
    lateral_start = (
        apply_block(side_blocks[0], sideways[:, :-2])
        + apply_block(side_blocks[1], sideways[:, 2:])
        + z_terms(side_blocks, start, depth)
    )
    drive_f = rhs - lateral_start - apply_block(x_upper, ahead)
    prefix = prefix_2(
        compose_planes(drive_f, x_lower, depth, upward),
        "gx",
        combine,
        neutral_map(rows, depth, species),
        False,
    )
    entering = prefix[1]
    forward = run_planes(drive_f, x_lower, entering, upward)
    widened = padded(forward, (("gy", 1),), 1)
    lateral_forward = (
        apply_block(side_blocks[0], widened[:, :-2])
        + apply_block(side_blocks[1], widened[:, 2:])
        + z_terms(side_blocks, forward, depth)
    )
    behind = jnp.concatenate([entering[None], forward[:-1]], 0)
    drive_b = rhs - lateral_forward - apply_block(x_lower, behind)
    suffix = prefix_2(
        compose_planes(drive_b, x_upper, depth, downward),
        "gx",
        combine,
        neutral_map(rows, depth, species),
        True,
    )
    arriving = suffix[1]
    result = run_planes(drive_b, x_upper, arriving, downward)
    return (forward, result)


def solution(mesh):
    return jax.shard_map(
        local,
        mesh=mesh,
        in_specs=(
            P("gx", "gy", None),
            P("gx", "gy", None),
            P("gx", "gy", None, None),
            P("gx", "gy", None, None),
            P("gx", "gy", None, None),
            P(None, "gx", "gy", None, None),
        ),
        out_specs=(P("gx", "gy", None), P("gx", "gy", None)),
        check_vma=False,
    )
```

profile of v0, /device:TPU:96, one launch (start us, length us, event | category | flops | bytes accessed | tf_op | source)
XLA Modules:
  0.0 351.1 jit_solution(17718955051626670756)
XLA Ops:
  7.3 1.0 fusion.4
  10.0 1.0 fusion.3
  12.6 5.0 %collective-permute-start = (f32[2,1,1024]{2,1,0:T(1,128)}, f32[2,1,1024]{2,1,0:T(1,128)S(1)}, u32[]{:S(2)}, u32[]{:S(2)}) collective-permute-start(f32[2,1,1024]{2,1,0:T(1,128)} %param.10), channel_id=1, source_target_pairs={{0,1},{1,2},{2,3},{3,4},{4,5},{5,6},{6,7},{7,8},{8,9},{9,10},{10,1... | collective-permute-start | bytes 24584 | tf_op jit(solution)/shard_map/ppermute | solution.py:12
  17.7 1.9 collective-permute-start.1
  20.3 1.3 collective-permute-start.2
  21.6 1.3 fusion.2
  24.1 2.3 reshape.531
  28.3 2.0 fusion.12
  30.3 1.4 reshape.543
  31.7 1.3 reshape.556
  34.3 2.0 fusion.17
  39.1 27.5 %all_gather.14 = f32[32,1,1024]{2,1,0:T(1,128)S(1)} all-gather(f32[1,1,1024]{2,1,0:T(1,128)S(1)} %sub.104), channel_id=1, replica_groups=mesh['gx'=32,'gy'=16] {'gx'}, dimensions={0}, use_global_device_ids=true | all-gather | bytes 135168 | tf_op jit(solution)/shard_map/all_gather | solution.py:30
  66.7 16.0 %all-gather.3.cloned.1.call-done = f32[32,1,16,4096]{3,2,1,0:T(8,128)} async-done(((f32[1,1,16,4096]{3,2,1,0:T(8,128)}), f32[32,1,16,4096]{3,2,1,0:T(8,128)}) %all-gather.3.cloned.1.call-update) | async-done | bytes 8388624 | tf_op jit(solution)/shard_map/all_gather | solution.py:30
  86.6 2.4 collective-permute-start.4
  89.0 4.9 %collective-permute-start.3 = (f32[2,1,1024]{2,1,0:T(1,128)S(1)}, f32[2,1,1024]{2,1,0:T(1,128)S(1)}, u32[]{:S(2)}, u32[]{:S(2)}) collective-permute-start(f32[2,1,1024]{2,1,0:T(1,128)S(1)} %pad_maximum_fusion.1), channel_id=1, source_target_pairs={{0,1},{1,2},{2,3},{3,4},{4,5},{5,6},{6,7},{7,8},{8,9},{9,10},{10,1... | collective-permute-start | bytes 24584 | tf_op jit(solution)/shard_map/ppermute | solution.py:12
  95.9 2.0 fusion.26
  99.1 2.0 fusion.22
  102.5 134.0 %all_gather.16 = f32[32,1,1024]{2,1,0:T(1,128)S(1)} all-gather(f32[1,1,1024]{2,1,0:T(1,128)S(1)} %sub.111), channel_id=1, replica_groups=mesh['gx'=32,'gy'=16] {'gx'}, dimensions={0}, use_global_device_ids=true | all-gather | bytes 135168 | tf_op jit(solution)/shard_map/all_gather | solution.py:30
  236.4 105.2 %while.27 = (s32[]{:T(128)}, f32[1,1024]{1,0:T(1,128)S(1)}, s32[]{:T(128)}, f32[32,1,1024]{2,1,0:T(1,128)S(1)}, f32[32,1,16,4096]{3,2,1,0:T(8,128)}, /*index=5*/...) while((s32[]{:T(128)}, f32[1,1024]{1,0:T(1,128)S(1)}, s32[]{:T(128)}, f32[32,1,1024]{2,1,0:T(1,128)S(1)}, ...), condition=%wide.region_3.4_spmd, body=%wide.region_2.3_spmd.sunk | while | flops 787462 | bytes 1355943 | solution.py:39
  239.8 1.0 constant_dynamic-slice_fusion.5
  243.2 1.0 constant_dynamic-slice_fusion.5
  246.6 1.0 constant_dynamic-slice_fusion.5
  263.6 1.0 constant_dynamic-slice_fusion.5
  267.0 1.0 constant_dynamic-slice_fusion.5
  (352 shorter events, 121.2 us)
Async XLA Ops:
  7.2 24.5 %copy-start.1 = (bf16[2,1,16,4096]{3,2,1,0:T(8,128)(2,1)S(1)}, bf16[2,1,16,4096]{3,2,1,0:T(8,128)(2,1)}, u32[]{:S(2)}) copy-start(bf16[2,1,16,4096]{3,2,1,0:T(8,128)(2,1)} %param.13) | copy-start | bytes 786436
  7.2 23.1 %copy-start = (bf16[2,1,16,4096]{3,2,1,0:T(8,128)(2,1)S(1)}, bf16[2,1,16,4096]{3,2,1,0:T(8,128)(2,1)}, u32[]{:S(2)}) copy-start(bf16[2,1,16,4096]{3,2,1,0:T(8,128)(2,1)} %param.14) | copy-start | bytes 786436
  7.2 16.2 %copy-start.5 = (f32[2,1,1024]{2,1,0:T(1,128)S(1)}, f32[2,1,1024]{2,1,0:T(1,128)}, u32[]{:S(2)}) copy-start(f32[2,1,1024]{2,1,0:T(1,128)} %param.10) | copy-start | bytes 24580
  7.2 19.2 %copy-start.6 = (f32[2,1,1024]{2,1,0:T(1,128)S(1)}, f32[2,1,1024]{2,1,0:T(1,128)}, u32[]{:S(2)}) copy-start(f32[2,1,1024]{2,1,0:T(1,128)} %param.11) | copy-start | bytes 24580
  7.2 75.5 %all-gather.3.cloned.1.call-start = ((), (), s32[]{:S(2)}) async-start(), calls=%async_computation | async-start | bytes 8650752 | tf_op jit(solution)/shard_map/all_gather | solution.py:30
  9.9 226.5 %all-gather.5.cloned.1.call-start = ((), (), s32[]{:S(2)}) async-start(), calls=%async_computation.1 | async-start | bytes 8650752 | tf_op jit(solution)/shard_map/all_gather | solution.py:30
  12.6 23.6 %collective-permute-start = (f32[2,1,1024]{2,1,0:T(1,128)}, f32[2,1,1024]{2,1,0:T(1,128)S(1)}, u32[]{:S(2)}, u32[]{:S(2)}) collective-permute-start(f32[2,1,1024]{2,1,0:T(1,128)} %param.10), channel_id=1, source_target_pairs={{0,1},{1,2},{2,3},{3,4},{4,5},{5,6},{6,7},{7,8},{8,9},{9,10},{10,1... | collective-permute-start | bytes 24584 | tf_op jit(solution)/shard_map/ppermute | solution.py:12
  17.7 18.7 %collective-permute-start.1 = (f32[2,1,1024]{2,1,0:T(1,128)}, f32[2,1,1024]{2,1,0:T(1,128)S(1)}, u32[]{:S(2)}, u32[]{:S(2)}) collective-permute-start(f32[2,1,1024]{2,1,0:T(1,128)} %param.10), channel_id=1, source_target_pairs={{1,0},{2,1},{3,2},{4,3},{5,4},{6,5},{7,6},{8,7},{9,8},{10,9},{11,1... | collective-permute-start | bytes 24584 | tf_op jit(solution)/shard_map/ppermute | solution.py:15
  20.3 13.8 %collective-permute-start.2 = (f32[1,1,1024]{2,1,0:T(1,128)S(1)}, f32[1,1,1024]{2,1,0:T(1,128)S(1)}, u32[]{:S(2)}, u32[]{:S(2)}) collective-permute-start(f32[1,1,1024]{2,1,0:T(1,128)S(1)} %get-tuple-element.173), channel_id=1, source_target_pairs={{16,0},{32,16},{48,32},{64,48},{80,64},{96,80},{112,96},{128,112},... | collective-permute-start | bytes 12296 | tf_op jit(solution)/shard_map/ppermute | solution.py:23
  30.3 8.8 %copy-start.4 = (f32[2,16,1,64]{3,2,1,0:T(1,128)}, f32[2,16,1,64]{3,2,1,0:T(1,128)S(1)}, u32[]{:S(2)}) copy-start(f32[2,16,1,64]{3,2,1,0:T(1,128)S(1)} %fusion.12) | copy-start | bytes 24580
  33.6 49.1 %copy-start.2 = (bf16[2,16,64,64]{3,2,1,0:T(8,128)(2,1)}, bf16[2,16,64,64]{3,2,1,0:T(8,128)(2,1)S(1)}, u32[]{:S(2)}) copy-start(bf16[2,16,64,64]{3,2,1,0:T(8,128)(2,1)S(1)} %reshape.533) | copy-start | bytes 786436
  38.3 44.3 %copy-start.3 = (f32[2,16,64]{2,1,0:T(8,128)}, f32[2,16,64]{2,1,0:T(8,128)S(1)}, u32[]{:S(2)}) copy-start(f32[2,16,64]{2,1,0:T(8,128)S(1)} %subtract_subtract_fusion.1) | copy-start | bytes 24580
  86.5 257.7 %copy-start.7 = (f32[2,1,1024]{2,1,0:T(1,128)}, f32[2,1,1024]{2,1,0:T(1,128)S(1)}, u32[]{:S(2)}) copy-start(f32[2,1,1024]{2,1,0:T(1,128)S(1)} %pad_maximum_fusion.1) | copy-start | bytes 24580
  86.6 11.3 %collective-permute-start.4 = (f32[2,1,1024]{2,1,0:T(1,128)S(1)}, f32[2,1,1024]{2,1,0:T(1,128)S(1)}, u32[]{:S(2)}, u32[]{:S(2)}) collective-permute-start(f32[2,1,1024]{2,1,0:T(1,128)S(1)} %pad_maximum_fusion.1), channel_id=1, source_target_pairs={{1,0},{2,1},{3,2},{4,3},{5,4},{6,5},{7,6},{8,7},{9,8},{10,9},{11,1... | collective-permute-start | bytes 24584 | tf_op jit(solution)/shard_map/ppermute | solution.py:15
  89.0 9.1 %collective-permute-start.3 = (f32[2,1,1024]{2,1,0:T(1,128)S(1)}, f32[2,1,1024]{2,1,0:T(1,128)S(1)}, u32[]{:S(2)}, u32[]{:S(2)}) collective-permute-start(f32[2,1,1024]{2,1,0:T(1,128)S(1)} %pad_maximum_fusion.1), channel_id=1, source_target_pairs={{0,1},{1,2},{2,3},{3,4},{4,5},{5,6},{6,7},{7,8},{8,9},{9,10},{10,1... | collective-permute-start | bytes 24584 | tf_op jit(solution)/shard_map/ppermute | solution.py:12
Sparse Core Ops, SparseCore 0:
  11.2 71.4 all-gather.2
  85.8 67.7 all-gather.4
where the time goes:
time: 353 us; the launch traced here: 351 us
  blocking collectives  161 us (46%)
  local copies, waits for them, and re-layouts  72.8 us (21%)
  matrix products  46.3 us (13%)
  other arithmetic  22.9 us (6%)
  waiting for transfers between devices  16 us (5%)
  starting transfers between devices  15.6 us (4%)
  between operations  14.4 us (4%)
    all_gather x2, blocking collectives, prefix_2(): gathered = jax.tree.map(lambda a: lax.all_gather(a, axis), part)  161 us
    dot_general x48, matrix products, apply_block(): jnp.einsum('...zab,...zb->...za', matrix, column, precision=lax.Precision...  45.9 us
    another operation x114, local copies, waits for them, and re-layouts  32.7 us
    dynamic_slice x31, local copies, waits for them, and re-layouts, one(): lax.dynamic_index_in_dim(a, source, 0, False)  30.1 us
    another operation x31, other arithmetic  18 us
    all_gather x2, waiting for transfers between devices, prefix_2(): gathered = jax.tree.map(lambda a: lax.all_gather(a, axis), part)  16 us
    ppermute x2, starting transfers between devices, padded(): lax.ppermute(lax.slice_in_dim(block, block.shape[dim] - width, None, axis...  9.89 us
  transfers between devices with their start and end apart: 7, of which 1 were waited for; matrix products, arithmetic and copies ran while one was open for 9% of the time, Pallas kernels for 0%

commit v1 on v0

v1 whole, which is shorter than its diff:
```python
import functools

import jax
import jax.numpy as jnp
from jax import lax
from jax.experimental import pallas as pl
from jax.experimental.pallas import tpu as pltpu
from jax.sharding import PartitionSpec as P

MESH = pl.DeviceIdType.MESH
F32 = jnp.float32
BF16 = jnp.bfloat16
CHUNK = 8


def lane_of(shape):
    return lax.broadcasted_iota(jnp.int32, shape, len(shape) - 1)


def row_of(shape):
    return lax.broadcasted_iota(jnp.int32, shape, len(shape) - 2)


def swap_halves(x):
    return pltpu.roll(x, 64, 1)


def kernel(nx, ny, nz, *refs):
    (start, source, diag, lower, upper, side, forward_out, result_out,
     v_start, v_source, v_diag, v_lower, v_upper, v_side,
     halo_dn, halo_up, ahead, pad, spread, cells, m_f, m_b, m_in, b_f, b_b, b_in, state, e_f, e_b,
     f_mine, f_dn, f_up,
     load_sem, halo_send, halo_recv, m_send, m_recv, b_send, b_recv, e_send, e_recv, f_send, f_recv) = refs
    me, my = lax.axis_index("gx"), lax.axis_index("gy")
    core, chip = lax.rem(me, 2), lax.div(me, 2)
    low, high, before = my > 0, my < ny - 1, me > 0
    last = me == nx - 1

    barrier = pltpu.get_barrier_semaphore()

    @pl.when(low)
    def _():
        pl.semaphore_signal(barrier, inc=1, device_id=(me, my - 1), device_id_type=MESH)

    @pl.when(high)
    def _():
        pl.semaphore_signal(barrier, inc=1, device_id=(me, my + 1), device_id_type=MESH)

    def greet(i, carry):
        pl.semaphore_signal(barrier, inc=1, device_id=(lax.rem(me + i, nx), my), device_id_type=MESH)
        return carry

    lax.fori_loop(1, nx, greet, 0)

    loads = [pltpu.make_async_copy(a, b, load_sem.at[i]) for i, (a, b) in enumerate(
        ((start, v_start), (lower, v_lower), (source, v_source), (diag, v_diag), (side, v_side), (upper, v_upper)))]
    for load in loads:
        load.start()

    def widen(x, top):
        lanes = lane_of(x.shape)
        turned = swap_halves(x)
        spread[pl.ds(top, 8 * nz // 16, stride=2), :] = jnp.where(lanes < 64, x, turned)
        spread[pl.ds(top + 1, 8 * nz // 16, stride=2), :] = jnp.where(lanes < 64, turned, x)
        return spread[top:top + nz, :]

    def narrow(x):
        spread[0:nz, :] = x
        even = spread[pl.ds(0, nz // 2, stride=2), :]
        odd = spread[pl.ds(1, nz // 2, stride=2), :]
        return jnp.where(lane_of(even.shape) < 64, even, odd)

    def shifted(x):
        pad[8:8 + nz, :] = x
        return pad[7:7 + nz, :], pad[9:9 + nz, :]

    pad[...] = jnp.zeros_like(pad)

    pick = jnp.where(lax.div(lax.rem(row_of((256, 128)), 128), 64) == lax.rem(lane_of((256, 128)), 2), 1.0, 0.0).astype(BF16)

    def apply(terms):
        out = jnp.zeros((nz, 128), F32)
        lanes = lax.div(lax.rem(lane_of((nz, 128)), 64), 2)
        for base in range(0, 32, CHUNK):
            pieces = []
            for c in range(base, base + CHUNK):
                total = None
                for block, vector in terms:
                    term = block[:, c * 128:(c + 1) * 128].astype(F32) * vector
                    total = term if total is None else total + term
                pieces.append(total)
            flat = jnp.concatenate(pieces, axis=0)
            high_part = flat.astype(BF16)
            low_part = (flat - high_part.astype(F32)).astype(BF16)
            sums = jnp.dot(jnp.concatenate([high_part, low_part], axis=1), pick, preferred_element_type=F32)
            for i in range(CHUNK):
                out = jnp.where(lanes == base + i, sums[i * nz:(i + 1) * nz, :], out)
        return out

    def square(z, slot):
        return cells[pl.ds(slot * 32 * nz + z, 32, stride=nz), :]

    def lay_out(block, slot, by=None):
        for c in range(32):
            piece = block[:, c * 128:(c + 1) * 128]
            piece = piece.astype(F32) if by is None else jnp.dot(piece, by, preferred_element_type=F32)
            cells[slot * 32 * nz + c * nz:slot * 32 * nz + (c + 1) * nz, :] = piece

    source_lane = row_of((128, 128))
    target = lax.div(source_lane, 64) * 64 + lax.rem(source_lane, 2) * 32 + lax.div(lax.rem(source_lane, 64), 2)
    sort = jnp.where(target == lane_of((128, 128)), 1.0, 0.0).astype(BF16)

    def compose(later, earlier, out):
        lay_out(later, 0, sort)
        lay_out(earlier, 1)
        lanes = lane_of((32, 128))
        for z in range(nz):
            b = square(z, 1)
            turned = swap_halves(b)
            right = jnp.concatenate([
                jnp.where(lanes < 64, b, 0.0), jnp.where(lanes < 64, turned, 0.0),
                jnp.where(lanes < 64, 0.0, turned), jnp.where(lanes < 64, 0.0, b)], axis=0).astype(BF16)
            out[z] = jnp.dot(square(z, 0).astype(BF16), right, preferred_element_type=F32)

    def compose_both(later, earlier, out, flip):
        @pl.when(jnp.logical_not(flip))
        def _():
            compose(later, earlier, out)

        @pl.when(flip)
        def _():
            compose_turned(later, earlier, out)

    order = jnp.where(lax.div(lane_of((64, 64)), 2) + 32 * lax.rem(lane_of((64, 64)), 2) == row_of((64, 64)), 1.0, 0.0).astype(BF16)

    unorder = jnp.where(lax.div(row_of((64, 64)), 2) + 32 * lax.rem(row_of((64, 64)), 2) == lane_of((64, 64)), 1.0, 0.0).astype(BF16)

    def compose_turned(later, earlier, out):
        lay_out(later, 0, sort)
        lay_out(earlier, 1)
        nt = (((1,), (1,)), ((), ()))
        for z in range(nz):
            a, b = square(z, 0), square(z, 1)
            a_stack = jnp.concatenate([a[:, :64], swap_halves(a)[:, :64]], axis=0).astype(BF16)
            b_stack = jnp.concatenate([b[:, :64], swap_halves(b)[:, :64]], axis=0).astype(BF16)
            b_turned = lax.dot_general(order, b_stack, nt, preferred_element_type=F32).astype(BF16)
            a_rows = jnp.dot(unorder, a_stack, preferred_element_type=F32).astype(BF16)
            turned = lax.dot_general(b_turned, a_rows, nt, preferred_element_type=F32)
            out[z] = jnp.concatenate([turned[:32], turned[32:]], axis=1)

    loads[1].wait()
    compose_both(v_lower.at[1], v_lower.at[0], m_f, core == 1)
    loads[0].wait()
    pl.semaphore_wait(barrier, nx - 1 + low.astype(jnp.int32) + high.astype(jnp.int32))

    def copy(src, dst, send, recv, where):
        return pltpu.make_async_remote_copy(src_ref=src, dst_ref=dst, send_sem=send, recv_sem=recv,
                                            device_id=where, device_id_type=MESH)

    @pl.when(low)
    def _():
        copy(v_start, halo_up, halo_send.at[0], halo_recv.at[0], (me, my - 1)).start()

    @pl.when(high)
    def _():
        copy(v_start, halo_dn, halo_send.at[1], halo_recv.at[1], (me, my + 1)).start()

    @pl.when(before)
    def _():
        copy(v_start.at[0], ahead, halo_send.at[2], halo_recv.at[2], (me - 1, my)).start()

    def to_owners(rows, inbox, slot, side_core, index, send, recv):
        def one(i, carry):
            z = lax.rem(chip + i, nz)
            owner = 2 * z + side_core

            @pl.when(owner != me)
            def _():
                copy(rows.at[z], inbox.at[slot], send.at[index], recv.at[index], (owner, my)).start()

            @pl.when(owner == me)
            def _():
                pltpu.make_async_copy(rows.at[z], inbox.at[slot], recv.at[index]).start()

            return carry

        lax.fori_loop(0, nz, one, 0)

    def from_owner(boxes, side_core, index):
        def one(step, carry):
            to = step if side_core == 0 else nx - 1 - step

            @pl.when(to != me)
            def _():
                copy(state.at[step], boxes.at[chip], e_send, e_recv.at[index], (to, my)).start()

            @pl.when(to == me)
            def _():
                pltpu.make_async_copy(state.at[step], boxes.at[chip], e_recv.at[index]).start()

            return carry

        lax.fori_loop(0, nx, one, 0)

    def landed(ref, sem):
        pltpu.make_async_copy(ref, ref, sem).wait()

    slot_f, slot_b = me, nx - 1 - me
    to_owners(m_f, m_in, slot_f, 0, 0, m_send, m_recv)

    loads[2].wait()
    loads[3].wait()
    loads[4].wait()
    loads[5].wait()
    mine = [widen(v_start[p], 0) for p in range(2)]
    rhs = [apply([(v_diag.at[p], widen(v_source[p], 0))]) for p in range(2)]
    compose_both(v_upper.at[0], v_upper.at[1], m_b, core == 0)

    @pl.when(jnp.logical_not(low))
    def _():
        halo_dn[...] = jnp.zeros_like(halo_dn)

    @pl.when(jnp.logical_not(high))
    def _():
        halo_up[...] = jnp.zeros_like(halo_up)

    @pl.when(last)
    def _():
        ahead[...] = jnp.zeros_like(ahead)

    @pl.when(high)
    def _():
        landed(halo_up, halo_recv.at[0])

    @pl.when(low)
    def _():
        landed(halo_dn, halo_recv.at[1])

    @pl.when(jnp.logical_not(last))
    def _():
        landed(ahead, halo_recv.at[2])

    next_plane = [mine[1], widen(ahead[...], 0)]
    fixed, drive = [], []
    for p in range(2):
        below, above = shifted(mine[p])
        fixed.append(apply([(v_side.at[0, p], widen(halo_dn[p], 0)), (v_side.at[1, p], widen(halo_up[p], 0)),
                            (v_side.at[2, p], below), (v_side.at[3, p], above), (v_upper.at[p], next_plane[p])]))
        drive.append(rhs[p] - fixed[p])

    def put(rows, value):
        for z in range(nz):
            rows[z] = value[z:z + 1, :]

    def take(boxes, which):
        return jnp.concatenate([boxes[z, which] for z in range(nz)], axis=0)

    put(b_f, drive[1] - apply([(v_lower.at[1], drive[0])]))
    to_owners(b_f, b_in, slot_f, 0, 0, b_send, b_recv)
    to_owners(m_b, m_in, slot_b, 1, 1, m_send, m_recv)

    def chain(boxes, side_core):
        index = side_core
        landed(m_in, m_recv.at[index])
        landed(b_in, b_recv.at[index])
        lanes = lane_of((32, 128))
        rows = row_of((32, 128))
        left = lanes < 64
        even_place = lax.rem(lanes, 64) == 2 * rows
        odd_place = lax.rem(lanes, 64) == 2 * rows + 1

        def pair(j, x):
            a, b = m_in[2 * j], jnp.broadcast_to(b_in[2 * j], (32, 128))
            x_rows = jnp.broadcast_to(x, (32, 128))
            even = jnp.sum(jnp.where(left, a * x_rows, 0.0) + jnp.where(jnp.logical_and(left, even_place), b, 0.0),
                           axis=1, keepdims=True)
            odd = jnp.sum(jnp.where(left, 0.0, a * x_rows) + jnp.where(jnp.logical_and(left, odd_place), b, 0.0),
                          axis=1, keepdims=True)
            even, odd = jnp.broadcast_to(even, (32, 128)), jnp.broadcast_to(odd, (32, 128))
            middle = jnp.sum(jnp.where(even_place, even, jnp.where(odd_place, odd, 0.0)), axis=0, keepdims=True)
            state[2 * j, 1] = middle
            state[2 * j + 1, 0] = middle
            t = jnp.sum(m_in[2 * j + 1] * jnp.where(left, even, odd), axis=0, keepdims=True)
            y = t + swap_halves(t) + b_in[2 * j + 1]
            state[2 * j, 0] = x
            state[2 * j + 1, 1] = y
            return y

        zero = jnp.zeros((1, 128), F32)
        lax.fori_loop(0, nx // 2, pair, zero)
        from_owner(boxes, side_core, index)

    @pl.when(core == 0)
    def _():
        chain(e_f, 0)

    landed(e_f, e_recv.at[0])
    f = [drive[0] - apply([(v_lower.at[0], take(e_f, 0))]), take(e_f, 1)]
    for p in range(2):
        f_mine[p] = f[p]

    @pl.when(low)
    def _():
        copy(f_mine, f_up, f_send.at[0], f_recv.at[0], (me, my - 1)).start()

    @pl.when(high)
    def _():
        copy(f_mine, f_dn, f_send.at[1], f_recv.at[1], (me, my + 1)).start()

    @pl.when(jnp.logical_not(low))
    def _():
        f_dn[...] = jnp.zeros_like(f_dn)

    @pl.when(jnp.logical_not(high))
    def _():
        f_up[...] = jnp.zeros_like(f_up)

    partial = []
    for p in range(2):
        forward_out[p] = narrow(f[p])
        below, above = shifted(f[p])
        partial.append(fixed[p] + f[p] - apply([(v_side.at[2, p], below), (v_side.at[3, p], above)]))

    @pl.when(high)
    def _():
        landed(f_up, f_recv.at[0])

    @pl.when(low)
    def _():
        landed(f_dn, f_recv.at[1])

    g = [partial[p] - apply([(v_side.at[0, p], f_dn[p]), (v_side.at[1, p], f_up[p])]) for p in range(2)]
    put(b_b, g[0] - apply([(v_upper.at[0], g[1])]))
    to_owners(b_b, b_in, slot_b, 1, 1, b_send, b_recv)

    @pl.when(core == 1)
    def _():
        chain(e_b, 1)

    landed(e_b, e_recv.at[1])
    result_out[0] = narrow(take(e_b, 1))
    result_out[1] = narrow(g[1] - apply([(v_upper.at[1], take(e_b, 0))]))

    @pl.when(low)
    def _():
        landed(v_start, halo_send.at[0])
        landed(f_mine, f_send.at[0])

    @pl.when(high)
    def _():
        landed(v_start, halo_send.at[1])
        landed(f_mine, f_send.at[1])

    @pl.when(before)
    def _():
        landed(ahead, halo_send.at[2])

    for side_core in range(2):
        for rows, sem in (((m_f, m_b)[side_core], m_send), ((b_f, b_b)[side_core], b_send)):
            @pl.when(core == side_core)
            def _():
                landed(rows.at[pl.ds(0, nz - 1)], sem.at[side_core])

            @pl.when(core != side_core)
            def _():
                landed(rows, sem.at[side_core])

    landed(state.at[pl.ds(0, nx - 1)], e_send)


def solution(mesh):
    nx, ny = mesh.shape["gx"], mesh.shape["gy"]

    def local(start, source, diag, lower, upper, side):
        nz = lower.shape[2]
        half = nz // 2
        width = lower.shape[3]
        any_space = pl.BlockSpec(memory_space=pl.ANY)
        vmem = pl.BlockSpec(memory_space=pltpu.VMEM)
        out = jax.ShapeDtypeStruct((2, half, 128), F32)
        dma = pltpu.SemaphoreType.DMA
        forward, result = pl.pallas_call(
            functools.partial(kernel, nx, ny, nz),
            out_shape=(out, out),
            in_specs=[any_space] * 6,
            out_specs=(vmem, vmem),
            scratch_shapes=[
                pltpu.VMEM((2, half, 128), F32), pltpu.VMEM((2, half, 128), F32),
                pltpu.VMEM((2, nz, width), BF16), pltpu.VMEM((2, nz, width), BF16), pltpu.VMEM((2, nz, width), BF16),
                pltpu.VMEM((4, 2, nz, width), BF16),
                pltpu.VMEM((2, half, 128), F32), pltpu.VMEM((2, half, 128), F32), pltpu.VMEM((half, 128), F32),
                pltpu.VMEM((nz + 16, 128), F32), pltpu.VMEM((nz, 128), F32), pltpu.VMEM((2 * 32 * nz, 128), F32),
                pltpu.VMEM((nz, 32, 128), F32), pltpu.VMEM((nz, 32, 128), F32), pltpu.VMEM((nx, 32, 128), F32),
                pltpu.VMEM((nz, 1, 128), F32), pltpu.VMEM((nz, 1, 128), F32), pltpu.VMEM((nx, 1, 128), F32),
                pltpu.VMEM((nx, 2, 1, 128), F32),
                pltpu.VMEM((nz, 2, 1, 128), F32), pltpu.VMEM((nz, 2, 1, 128), F32),
                pltpu.VMEM((2, nz, 128), F32), pltpu.VMEM((2, nz, 128), F32), pltpu.VMEM((2, nz, 128), F32),
                dma((6,)), dma((3,)), dma((3,)), dma((2,)), dma((2,)), dma((2,)), dma((2,)), dma, dma((2,)),
                dma((2,)), dma((2,)),
            ],
            compiler_params=pltpu.CompilerParams(collective_id=0, has_side_effects=True),
        )(start.reshape(2, half, 128), source.reshape(2, half, 128), diag.reshape(2, nz, width),
          lower.reshape(2, nz, width), upper.reshape(2, nz, width), side.reshape(4, 2, nz, width))
        return forward.reshape(start.shape), result.reshape(start.shape)

    return jax.shard_map(
        local,
        mesh=mesh,
        in_specs=(P("gx", "gy", None), P("gx", "gy", None), P("gx", "gy", None, None), P("gx", "gy", None, None),
                  P("gx", "gy", None, None), P(None, "gx", "gy", None, None)),
        out_specs=(P("gx", "gy", None), P("gx", "gy", None)),
        check_vma=False,
    )
```

time: 353 us -> 43.9 us (0.12)
  the two profiles are of different devices: /device:TPU:96 before, /device:TPU:193 now
where the time goes in v1:
time: 43.9 us; the launch traced here: 43.7 us
  Pallas kernels  41.2 us (94%)
  local copies, waits for them, and re-layouts  1.9 us (4%)
  between operations  0.65 us (1%)
    pallas_call x1, Pallas kernels, local(): pl.pallas_call(functools.partial(kernel, nx, ny, nz), out_shape=(out, out...  41.2 us
    unnamed x4, local copies, waits for them, and re-layouts  1.9 us

profile of v1, /device:TPU:193, one launch (start us, length us, event | category | flops | bytes accessed | tf_op | source)
XLA Modules:
  0.0 43.7 jit_solution(16672209003674040623)
XLA Ops:
  0.6 41.2 %shard_map.77 = (f32[2,8,128]{2,1,0:T(8,128)}, f32[2,8,128]{2,1,0:T(8,128)}) custom-call(f32[2,8,128]{2,1,0:T(8,128)} %bitcast.12, f32[2,8,128]{2,1,0:T(8,128)} %bitcast.13, bf16[2,16,4096]{2,1,0:T(8,128)(2,1)} %bitcast.9, bf16[2,16,4096]{2,1,0:T(8,128)(2,1)} %bitcast.10, bf16[2,16,4096]{2,1,0:T(8,128)(2,1)} %bitcast.11, bf16[4,2,16,4096]{3,2,1,0:T(8,128)(2,1)} %bitcast.8), custom_call_target="tpu_custom_call" | custom-call | tf_op jit(solution)/shard_map/pallas_call | solution.py:382
  41.8 0.0 copy-start
  41.8 1.3 %copy.12 = f32[2,1,1024]{2,1,0:T(1,128)} copy(f32[2,1,1024]{2,1,0:T(1,128)} %bitcast.15) | data formatting | bytes 16384
  43.1 0.0 copy-done
  43.1 0.6 %copy.13 = f32[2,1,1024]{2,1,0:T(1,128)} copy(f32[2,1,1024]{2,1,0:T(1,128)S(1)} %bitcast.14) | data formatting | bytes 16384
Async XLA Ops:
  41.8 1.3 %copy-start = (f32[2,8,128]{2,1,0:T(8,128)S(1)}, f32[2,8,128]{2,1,0:T(8,128)}, u32[]{:S(2)}) copy-start(f32[2,8,128]{2,1,0:T(8,128)} %get-tuple-element.5) | copy-start | bytes 24580

commit v2 on v1

--- a/solution.py
+++ b/solution.py
@@ -28,12 +28,20 @@
 def kernel(nx, ny, nz, *refs):
     (start, source, diag, lower, upper, side, forward_out, result_out,
      v_start, v_source, v_diag, v_lower, v_upper, v_side,
-     halo_dn, halo_up, ahead, pad, spread, cells, m_f, m_b, m_in, b_f, b_b, b_in, state, e_f, e_b,
+     halo_dn, halo_up, ahead, pad, spread, cells, m_f, m_b, m_in, b_f, b_b, b_in, state, e_f, e_b, m_odd,
      f_mine, f_dn, f_up,
-     load_sem, halo_send, halo_recv, m_send, m_recv, b_send, b_recv, e_send, e_recv, f_send, f_recv) = refs
+     load_sem, halo_send, halo_recv, m_send, m_recv, b_send, b_recv, e_send, e_recv, f_send, f_recv,
+     hello) = refs
     me, my = lax.axis_index("gx"), lax.axis_index("gy")
     core, chip = lax.rem(me, 2), lax.div(me, 2)
     low, high, before = my > 0, my < ny - 1, me > 0
+    edge = 4 if nz == 16 else 2
+
+    def opposite(place):
+        half = edge // 2
+        return lax.rem(lax.div(place, edge) + half, edge) * edge + lax.rem(lax.rem(place, edge) + half, edge)
+
+    line = jnp.where(core == 0, chip, opposite(chip))
     last = me == nx - 1
 
     barrier = pltpu.get_barrier_semaphore()
@@ -46,11 +54,16 @@
     def _():
         pl.semaphore_signal(barrier, inc=1, device_id=(me, my + 1), device_id_type=MESH)
 
-    def greet(i, carry):
-        pl.semaphore_signal(barrier, inc=1, device_id=(lax.rem(me + i, nx), my), device_id_type=MESH)
-        return carry
-
-    lax.fori_loop(1, nx, greet, 0)
+    def greet(semaphore):
+        def one(i, carry):
+            pl.semaphore_signal(semaphore, inc=1, device_id=(lax.rem(me + i, nx), my), device_id_type=MESH)
+            return carry
+
+        lax.fori_loop(1, nx, one, 0)
+
+    @pl.when(before)
+    def _():
+        greet(barrier)
 
     loads = [pltpu.make_async_copy(a, b, load_sem.at[i]) for i, (a, b) in enumerate(
         ((start, v_start), (lower, v_lower), (source, v_source), (diag, v_diag), (side, v_side), (upper, v_upper)))]
@@ -148,10 +161,19 @@
             turned = lax.dot_general(b_turned, a_rows, nt, preferred_element_type=F32)
             out[z] = jnp.concatenate([turned[:32], turned[32:]], axis=1)
 
-    loads[1].wait()
-    compose_both(v_lower.at[1], v_lower.at[0], m_f, core == 1)
+    @pl.when(before)
+    def _():
+        loads[1].wait()
+        compose_both(v_lower.at[1], v_lower.at[0], m_f, core == 1)
+
+    pl.semaphore_wait(barrier, nx - 2 + low.astype(jnp.int32) + high.astype(jnp.int32) + (me == 0).astype(jnp.int32))
+
+    @pl.when(me == 0)
+    def _():
+        greet(hello)
+        loads[1].wait()
+
     loads[0].wait()
-    pl.semaphore_wait(barrier, nx - 1 + low.astype(jnp.int32) + high.astype(jnp.int32))
 
     def copy(src, dst, send, recv, where):
         return pltpu.make_async_remote_copy(src_ref=src, dst_ref=dst, send_sem=send, recv_sem=recv,
@@ -165,48 +187,72 @@
     def _():
         copy(v_start, halo_dn, halo_send.at[1], halo_recv.at[1], (me, my + 1)).start()
 
-    @pl.when(before)
+    @pl.when(me >= 2)
     def _():
         copy(v_start.at[0], ahead, halo_send.at[2], halo_recv.at[2], (me - 1, my)).start()
 
-    def to_owners(rows, inbox, slot, side_core, index, send, recv):
+    def to_owner(rows, index, z, owner, send, recv):
+        slot = slots[index]
+        inbox = (m_in if rows.shape[1] == 32 else b_in).at[index]
+
+        @pl.when(owner != me)
+        def _():
+            copy(rows.at[z], inbox.at[slot], send.at[index], recv.at[index], (owner, my)).start()
+
+        @pl.when(owner == me)
+        def _():
+            pltpu.make_async_copy(rows.at[z], inbox.at[slot], recv.at[index]).start()
+
+    def to_owners(rows, index, send, recv):
         def one(i, carry):
             z = lax.rem(chip + i, nz)
-            owner = 2 * z + side_core
-
-            @pl.when(owner != me)
-            def _():
-                copy(rows.at[z], inbox.at[slot], send.at[index], recv.at[index], (owner, my)).start()
-
-            @pl.when(owner == me)
-            def _():
-                pltpu.make_async_copy(rows.at[z], inbox.at[slot], recv.at[index]).start()
-
+            if index == 0:
+                to_owner(rows, index, z, 2 * z + 1, send, recv)
+            else:
+                to_owner(rows, index, z, 2 * z, send, recv)
+                to_owner(rows, index, z, 2 * opposite(z) + 1, send, recv)
             return carry
 
         lax.fori_loop(0, nz, one, 0)
 
-    def from_owner(boxes, side_core, index):
-        def one(step, carry):
-            to = step if side_core == 0 else nx - 1 - step
-
-            @pl.when(to != me)
-            def _():
-                copy(state.at[step], boxes.at[chip], e_send, e_recv.at[index], (to, my)).start()
-
-            @pl.when(to == me)
-            def _():
-                pltpu.make_async_copy(state.at[step], boxes.at[chip], e_recv.at[index]).start()
-
-            return carry
-
-        lax.fori_loop(0, nx, one, 0)
+    def from_owner(boxes, index):
+        half = edge // 2
+        near = []
+        for ry in range(edge):
+            for rx in range(edge):
+                hops = min(rx, edge - rx) + min(ry, edge - ry)
+                if index == 0 or hops < half or (hops == half and 1 <= rx <= half):
+                    near.append((-hops, ry, rx))
+        for hops, ry, rx in sorted(near):
+            there = lax.rem(lax.div(chip, edge) + ry, edge) * edge + lax.rem(lax.rem(chip, edge) + rx, edge)
+            for which in range(2):
+                to = 2 * there + which
+                step = to if index == 0 else nx - 1 - to
+                src, dst = state.at[index, step], boxes.at[chip if index == 0 else line]
+                if hops:
+                    copy(src, dst, e_send.at[index], e_recv.at[index], (to, my)).start()
+                else:
+                    @pl.when(core != which)
+                    def _():
+                        copy(src, dst, e_send.at[index], e_recv.at[index], (to, my)).start()
+
+                    @pl.when(core == which)
+                    def _():
+                        pltpu.make_async_copy(src, dst, e_recv.at[index]).start()
 
     def landed(ref, sem):
         pltpu.make_async_copy(ref, ref, sem).wait()
 
-    slot_f, slot_b = me, nx - 1 - me
-    to_owners(m_f, m_in, slot_f, 0, 0, m_send, m_recv)
+    slots = (me, nx - 1 - me)
+
+    @pl.when(before)
+    def _():
+        to_owners(m_f, 0, m_send, m_recv)
+
+    @pl.when(me == 1)
+    def _():
+        pl.semaphore_wait(hello, 1)
+        copy(v_start.at[0], ahead, halo_send.at[2], halo_recv.at[2], (me - 1, my)).start()
 
     loads[2].wait()
     loads[3].wait()
@@ -214,7 +260,6 @@
     loads[5].wait()
     mine = [widen(v_start[p], 0) for p in range(2)]
     rhs = [apply([(v_diag.at[p], widen(v_source[p], 0))]) for p in range(2)]
-    compose_both(v_upper.at[0], v_upper.at[1], m_b, core == 0)
 
     @pl.when(jnp.logical_not(low))
     def _():
@@ -256,41 +301,59 @@
         return jnp.concatenate([boxes[z, which] for z in range(nz)], axis=0)
 
     put(b_f, drive[1] - apply([(v_lower.at[1], drive[0])]))
-    to_owners(b_f, b_in, slot_f, 0, 0, b_send, b_recv)
-    to_owners(m_b, m_in, slot_b, 1, 1, m_send, m_recv)
-
-    def chain(boxes, side_core):
-        index = side_core
-        landed(m_in, m_recv.at[index])
-        landed(b_in, b_recv.at[index])
+    to_owners(b_f, 0, b_send, b_recv)
+
+    @pl.when(me >= 2)
+    def _():
+        pl.semaphore_wait(hello, 1)
+
+    compose_both(v_upper.at[0], v_upper.at[1], m_b, core == 0)
+    to_owners(m_b, 1, m_send, m_recv)
+
+    def chain(boxes, index):
+        if index == 0:
+            landed(m_in.at[0, pl.ds(0, nx - 1)], m_recv.at[0])
+            m_in[0, 0] = jnp.zeros((32, 128), F32)
+        else:
+            landed(m_in.at[1], m_recv.at[1])
         lanes = lane_of((32, 128))
         rows = row_of((32, 128))
         left = lanes < 64
         even_place = lax.rem(lanes, 64) == 2 * rows
         odd_place = lax.rem(lanes, 64) == 2 * rows + 1
+        left_row = lane_of((1, 128)) < 64
+
+        def double(j, carry):
+            a = m_in[index, 2 * j]
+            turned = swap_halves(a)
+            m_in[index, 2 * j] = jnp.where(left, a, turned)
+            m_odd[j] = jnp.where(left, turned, a)
+            return carry
+
+        lax.fori_loop(0, nx // 2, double, 0, unroll=4)
+        landed(b_in.at[index], b_recv.at[index])
 
         def pair(j, x):
-            a, b = m_in[2 * j], jnp.broadcast_to(b_in[2 * j], (32, 128))
+            b = jnp.broadcast_to(b_in[index, 2 * j], (32, 128))
             x_rows = jnp.broadcast_to(x, (32, 128))
-            even = jnp.sum(jnp.where(left, a * x_rows, 0.0) + jnp.where(jnp.logical_and(left, even_place), b, 0.0),
-                           axis=1, keepdims=True)
-            odd = jnp.sum(jnp.where(left, 0.0, a * x_rows) + jnp.where(jnp.logical_and(left, odd_place), b, 0.0),
-                          axis=1, keepdims=True)
+            even = jnp.sum(m_in[index, 2 * j] * x_rows
+                           + jnp.where(jnp.logical_and(left, even_place), b, 0.0), axis=1, keepdims=True)
+            odd = jnp.sum(m_odd[j] * x_rows
+                          + jnp.where(jnp.logical_and(left, odd_place), b, 0.0), axis=1, keepdims=True)
             even, odd = jnp.broadcast_to(even, (32, 128)), jnp.broadcast_to(odd, (32, 128))
+            y = (jnp.sum(m_in[index, 2 * j + 1] * jnp.where(left, even, odd), axis=0, keepdims=True)
+                 + jnp.where(left_row, b_in[index, 2 * j + 1], 0.0))
             middle = jnp.sum(jnp.where(even_place, even, jnp.where(odd_place, odd, 0.0)), axis=0, keepdims=True)
-            state[2 * j, 1] = middle
-            state[2 * j + 1, 0] = middle
-            t = jnp.sum(m_in[2 * j + 1] * jnp.where(left, even, odd), axis=0, keepdims=True)
-            y = t + swap_halves(t) + b_in[2 * j + 1]
-            state[2 * j, 0] = x
-            state[2 * j + 1, 1] = y
+            state[index, 2 * j, 0] = x + swap_halves(x)
+            state[index, 2 * j, 1] = middle
+            state[index, 2 * j + 1, 0] = middle
+            state[index, 2 * j + 1, 1] = y + swap_halves(y)
             return y
 
-        zero = jnp.zeros((1, 128), F32)
-        lax.fori_loop(0, nx // 2, pair, zero)
-        from_owner(boxes, side_core, index)
-
-    @pl.when(core == 0)
+        lax.fori_loop(0, nx // 2, pair, jnp.zeros((1, 128), F32), unroll=True)
+        from_owner(boxes, index)
+
+    @pl.when(core == 1)
     def _():
         chain(e_f, 0)
 
@@ -331,11 +394,8 @@
 
     g = [partial[p] - apply([(v_side.at[0, p], f_dn[p]), (v_side.at[1, p], f_up[p])]) for p in range(2)]
     put(b_b, g[0] - apply([(v_upper.at[0], g[1])]))
-    to_owners(b_b, b_in, slot_b, 1, 1, b_send, b_recv)
-
-    @pl.when(core == 1)
-    def _():
-        chain(e_b, 1)
+    to_owners(b_b, 1, b_send, b_recv)
+    chain(e_b, 1)
 
     landed(e_b, e_recv.at[1])
     result_out[0] = narrow(take(e_b, 1))
@@ -355,17 +415,28 @@
     def _():
         landed(ahead, halo_send.at[2])
 
-    for side_core in range(2):
-        for rows, sem in (((m_f, m_b)[side_core], m_send), ((b_f, b_b)[side_core], b_send)):
-            @pl.when(core == side_core)
-            def _():
-                landed(rows.at[pl.ds(0, nz - 1)], sem.at[side_core])
-
-            @pl.when(core != side_core)
-            def _():
-                landed(rows, sem.at[side_core])
-
-    landed(state.at[pl.ds(0, nx - 1)], e_send)
+    @pl.when(core == 1)
+    def _():
+        landed(m_f.at[pl.ds(0, nz - 1)], m_send.at[0])
+        landed(b_f.at[pl.ds(0, nz - 1)], b_send.at[0])
+        landed(state.at[0, pl.ds(0, nx - 1)], e_send.at[0])
+
+    @pl.when(core == 0)
+    def _():
+        landed(b_f, b_send.at[0])
+
+    @pl.when(jnp.logical_and(core == 0, before))
+    def _():
+        landed(m_f, m_send.at[0])
+
+    landed(m_in.at[1, pl.ds(0, nx - 1)], m_send.at[1])
+    landed(b_in.at[1, pl.ds(0, nx - 1)], b_send.at[1])
+    landed(state.at[1, pl.ds(0, nz - 1)], e_send.at[1])
+
+
+def hand_out(forward_in, result_in, forward_out, result_out):
+    forward_out[...] = forward_in[...]
+    result_out[...] = result_in[...]
 
 
 def solution(mesh):
@@ -390,17 +461,19 @@
                 pltpu.VMEM((4, 2, nz, width), BF16),
                 pltpu.VMEM((2, half, 128), F32), pltpu.VMEM((2, half, 128), F32), pltpu.VMEM((half, 128), F32),
                 pltpu.VMEM((nz + 16, 128), F32), pltpu.VMEM((nz, 128), F32), pltpu.VMEM((2 * 32 * nz, 128), F32),
-                pltpu.VMEM((nz, 32, 128), F32), pltpu.VMEM((nz, 32, 128), F32), pltpu.VMEM((nx, 32, 128), F32),
-                pltpu.VMEM((nz, 1, 128), F32), pltpu.VMEM((nz, 1, 128), F32), pltpu.VMEM((nx, 1, 128), F32),
-                pltpu.VMEM((nx, 2, 1, 128), F32),
-                pltpu.VMEM((nz, 2, 1, 128), F32), pltpu.VMEM((nz, 2, 1, 128), F32),
+                pltpu.VMEM((nz, 32, 128), F32), pltpu.VMEM((nz, 32, 128), F32), pltpu.VMEM((2, nx, 32, 128), F32),
+                pltpu.VMEM((nz, 1, 128), F32), pltpu.VMEM((nz, 1, 128), F32), pltpu.VMEM((2, nx, 1, 128), F32),
+                pltpu.VMEM((2, nx, 2, 1, 128), F32),
+                pltpu.VMEM((nz, 2, 1, 128), F32), pltpu.VMEM((nz, 2, 1, 128), F32), pltpu.VMEM((nx // 2, 32, 128), F32),
                 pltpu.VMEM((2, nz, 128), F32), pltpu.VMEM((2, nz, 128), F32), pltpu.VMEM((2, nz, 128), F32),
-                dma((6,)), dma((3,)), dma((3,)), dma((2,)), dma((2,)), dma((2,)), dma((2,)), dma, dma((2,)),
-                dma((2,)), dma((2,)),
+                dma((6,)), dma((3,)), dma((3,)), dma((2,)), dma((2,)), dma((2,)), dma((2,)), dma((2,)), dma((2,)),
+                dma((2,)), dma((2,)), pltpu.SemaphoreType.REGULAR,
             ],
             compiler_params=pltpu.CompilerParams(collective_id=0, has_side_effects=True),
         )(start.reshape(2, half, 128), source.reshape(2, half, 128), diag.reshape(2, nz, width),
           lower.reshape(2, nz, width), upper.reshape(2, nz, width), side.reshape(4, 2, nz, width))
+        forward, result = pl.pallas_call(
+            hand_out, out_shape=(out, out), in_specs=[vmem, vmem], out_specs=(vmem, vmem))(forward, result)
         return forward.reshape(start.shape), result.reshape(start.shape)
 
     return jax.shard_map(

time: 43.9 us -> 40.9 us (0.932)
  local copies, waits for them, and re-layouts: 1.9 us -> 0 us
  Pallas kernels: 41.2 us -> 40 us
    pallas_call x1, Pallas kernels: 41.2 us -> 38.7 us  [local(): pl.pallas_call(functools.partial(kernel, nx, ny, nz), out_shape=(out, out...]
    unnamed x4 -> x0, local copies, waits for them, and re-layouts: 1.9 us -> none
    pallas_call x0 -> x1, Pallas kernels: none -> 1.32 us  [local(): pl.pallas_call(hand_out, out_shape=(out, out), in_specs=[vmem, vmem], out...]
where the time goes in v2:
time: 40.9 us; the launch traced here: 40.7 us
  Pallas kernels  40 us (98%)
  between operations  0.64 us (2%)
    pallas_call x1, Pallas kernels, local(): pl.pallas_call(functools.partial(kernel, nx, ny, nz), out_shape=(out, out...  38.7 us
    pallas_call x1, Pallas kernels, local(): pl.pallas_call(hand_out, out_shape=(out, out), in_specs=[vmem, vmem], out...  1.32 us

profile of v2, /device:TPU:193, one launch (start us, length us, event | category | flops | bytes accessed | tf_op | source)
XLA Modules:
  0.0 40.7 jit_solution(16030665725302842648)
XLA Ops:
  0.6 38.7 %shard_map.77 = (f32[2,8,128]{2,1,0:T(8,128)}, f32[2,8,128]{2,1,0:T(8,128)}) custom-call(f32[2,8,128]{2,1,0:T(8,128)} %bitcast.12, f32[2,8,128]{2,1,0:T(8,128)} %bitcast.13, bf16[2,16,4096]{2,1,0:T(8,128)(2,1)} %bitcast.9, bf16[2,16,4096]{2,1,0:T(8,128)(2,1)} %bitcast.10, bf16[2,16,4096]{2,1,0:T(8,128)(2,1)} %bitcast.11, bf16[4,2,16,4096]{3,2,1,0:T(8,128)(2,1)} %bitcast.8), custom_call_target="tpu_custom_call" | custom-call | tf_op jit(solution)/shard_map/pallas_call | solution.py:453
  39.3 1.3 %shard_map.78 = (f32[2,8,128]{2,1,0:T(8,128)}, f32[2,8,128]{2,1,0:T(8,128)}) custom-call(f32[2,8,128]{2,1,0:T(8,128)} %get-tuple-element.6.forward_in, f32[2,8,128]{2,1,0:T(8,128)} %get-tuple-element.7.result_in), custom_call_target="tpu_custom_call" | custom-call | tf_op jit(solution)/shard_map/pallas_call | solution.py:475

commit v3 on v2

--- a/solution.py
+++ b/solution.py
@@ -191,54 +191,43 @@
     def _():
         copy(v_start.at[0], ahead, halo_send.at[2], halo_recv.at[2], (me - 1, my)).start()
 
-    def to_owner(rows, index, z, owner, send, recv):
-        slot = slots[index]
-        inbox = (m_in if rows.shape[1] == 32 else b_in).at[index]
-
-        @pl.when(owner != me)
-        def _():
-            copy(rows.at[z], inbox.at[slot], send.at[index], recv.at[index], (owner, my)).start()
-
-        @pl.when(owner == me)
-        def _():
-            pltpu.make_async_copy(rows.at[z], inbox.at[slot], recv.at[index]).start()
+    offsets = sorted(
+        (-min(rx, edge - rx) - min(ry, edge - ry), ry, rx) for ry in range(edge) for rx in range(edge))
+    half = edge // 2
+    near = [(hops, ry, rx) for hops, ry, rx in offsets if -hops < half or (-hops == half and 1 <= rx <= half)]
+
+    def beyond(ry, rx):
+        return lax.rem(lax.div(chip, edge) + ry, edge) * edge + lax.rem(lax.rem(chip, edge) + rx, edge)
+
+    def send_to(hops, which, src, dst, send, recv, to):
+        if hops:
+            copy(src, dst, send, recv, (to, my)).start()
+        else:
+            @pl.when(core != which)
+            def _():
+                copy(src, dst, send, recv, (to, my)).start()
+
+            @pl.when(core == which)
+            def _():
+                pltpu.make_async_copy(src, dst, recv).start()
 
     def to_owners(rows, index, send, recv):
-        def one(i, carry):
-            z = lax.rem(chip + i, nz)
+        inbox = (m_in if rows.shape[1] == 32 else b_in).at[index, slots[index]]
+        for hops, ry, rx in offsets:
+            there = beyond(ry, rx)
             if index == 0:
-                to_owner(rows, index, z, 2 * z + 1, send, recv)
+                send_to(hops, 1, rows.at[there], inbox, send.at[0], recv.at[0], 2 * there + 1)
             else:
-                to_owner(rows, index, z, 2 * z, send, recv)
-                to_owner(rows, index, z, 2 * opposite(z) + 1, send, recv)
-            return carry
-
-        lax.fori_loop(0, nz, one, 0)
+                send_to(hops, 0, rows.at[there], inbox, send.at[1], recv.at[1], 2 * there)
+                send_to(hops, 1, rows.at[opposite(there)], inbox, send.at[1], recv.at[1], 2 * there + 1)
 
     def from_owner(boxes, index):
-        half = edge // 2
-        near = []
-        for ry in range(edge):
-            for rx in range(edge):
-                hops = min(rx, edge - rx) + min(ry, edge - ry)
-                if index == 0 or hops < half or (hops == half and 1 <= rx <= half):
-                    near.append((-hops, ry, rx))
-        for hops, ry, rx in sorted(near):
-            there = lax.rem(lax.div(chip, edge) + ry, edge) * edge + lax.rem(lax.rem(chip, edge) + rx, edge)
+        box = boxes.at[chip if index == 0 else line]
+        for hops, ry, rx in (offsets if index == 0 else near):
             for which in range(2):
-                to = 2 * there + which
+                to = 2 * beyond(ry, rx) + which
                 step = to if index == 0 else nx - 1 - to
-                src, dst = state.at[index, step], boxes.at[chip if index == 0 else line]
-                if hops:
-                    copy(src, dst, e_send.at[index], e_recv.at[index], (to, my)).start()
-                else:
-                    @pl.when(core != which)
-                    def _():
-                        copy(src, dst, e_send.at[index], e_recv.at[index], (to, my)).start()
-
-                    @pl.when(core == which)
-                    def _():
-                        pltpu.make_async_copy(src, dst, e_recv.at[index]).start()
+                send_to(hops, which, state.at[index, step], box, e_send.at[index], e_recv.at[index], to)
 
     def landed(ref, sem):
         pltpu.make_async_copy(ref, ref, sem).wait()
@@ -452,7 +441,7 @@
         dma = pltpu.SemaphoreType.DMA
         forward, result = pl.pallas_call(
             functools.partial(kernel, nx, ny, nz),
-            out_shape=(out, out),
+            out_shape=(pltpu.VMEM((2, half, 128), F32), pltpu.VMEM((2, half, 128), F32)),
             in_specs=[any_space] * 6,
             out_specs=(vmem, vmem),
             scratch_shapes=[
@@ -472,6 +461,8 @@
             compiler_params=pltpu.CompilerParams(collective_id=0, has_side_effects=True),
         )(start.reshape(2, half, 128), source.reshape(2, half, 128), diag.reshape(2, nz, width),
           lower.reshape(2, nz, width), upper.reshape(2, nz, width), side.reshape(4, 2, nz, width))
+        forward = pltpu.with_memory_space_constraint(forward, pltpu.VMEM)
+        result = pltpu.with_memory_space_constraint(result, pltpu.VMEM)
         forward, result = pl.pallas_call(
             hand_out, out_shape=(out, out), in_specs=[vmem, vmem], out_specs=(vmem, vmem))(forward, result)
         return forward.reshape(start.shape), result.reshape(start.shape)

time: 40.9 us -> 39.2 us (0.958)
  Pallas kernels: 40 us -> 38.5 us
    pallas_call x1, Pallas kernels: 38.7 us -> 37.9 us  [local(): pl.pallas_call(functools.partial(kernel, nx, ny, nz), out_shape=(pltpu.VM...]
    pallas_call x1, Pallas kernels: 1.32 us -> 0.61 us  [local(): pl.pallas_call(hand_out, out_shape=(out, out), in_specs=[vmem, vmem], out...]
where the time goes in v3:
time: 39.2 us; the launch traced here: 39.1 us
  Pallas kernels  38.5 us (98%)
  between operations  0.64 us (2%)
    pallas_call x1, Pallas kernels, local(): pl.pallas_call(functools.partial(kernel, nx, ny, nz), out_shape=(pltpu.VM...  37.9 us

profile of v3, /device:TPU:193, one launch (start us, length us, event | category | flops | bytes accessed | tf_op | source)
XLA Modules:
  0.0 39.1 jit_solution(5040194729234225734)
XLA Ops:
  0.6 37.9 %shard_map.77 = (f32[2,8,128]{2,1,0:T(8,128)S(1)}, f32[2,8,128]{2,1,0:T(8,128)S(1)}) custom-call(f32[2,8,128]{2,1,0:T(8,128)} %bitcast.12, f32[2,8,128]{2,1,0:T(8,128)} %bitcast.13, bf16[2,16,4096]{2,1,0:T(8,128)(2,1)} %bitcast.9, bf16[2,16,4096]{2,1,0:T(8,128)(2,1)} %bitcast.10, bf16[2,16,4096]{2,1,0:T(8,128)(2,1)} %bitcast.11, bf16[4,2,16,4096]{3,2,1,0:T(8,128)(2,1)} %bitcast.8), custom_call_target="tpu_custom_call" | custom-call | tf_op jit(solution)/shard_map/pallas_call | solution.py:442
  38.5 0.6 %shard_map.78 = (f32[2,8,128]{2,1,0:T(8,128)}, f32[2,8,128]{2,1,0:T(8,128)}) custom-call(f32[2,8,128]{2,1,0:T(8,128)S(1)} %get-tuple-element.6.forward_in, f32[2,8,128]{2,1,0:T(8,128)S(1)} %get-tuple-element.7.result_in), custom_call_target="tpu_custom_call" | custom-call | tf_op jit(solution)/shard_map/pallas_call | solution.py:466

commit v4 on v3

--- a/solution.py
+++ b/solution.py
@@ -28,7 +28,7 @@
 def kernel(nx, ny, nz, *refs):
     (start, source, diag, lower, upper, side, forward_out, result_out,
      v_start, v_source, v_diag, v_lower, v_upper, v_side,
-     halo_dn, halo_up, ahead, pad, spread, cells, m_f, m_b, m_in, b_f, b_b, b_in, state, e_f, e_b, m_odd,
+     halo_dn, halo_up, ahead, pad, spread, cells, m_f, m_b, m_in, b_f, b_b, b_in, state, e_f, e_b, m_odd, k_f, k_b,
      f_mine, f_dn, f_up,
      load_sem, halo_send, halo_recv, m_send, m_recv, b_send, b_recv, e_send, e_recv, f_send, f_recv,
      hello) = refs
@@ -41,7 +41,11 @@
         half = edge // 2
         return lax.rem(lax.div(place, edge) + half, edge) * edge + lax.rem(lax.rem(place, edge) + half, edge)
 
-    line = jnp.where(core == 0, chip, opposite(chip))
+    def line_at(place):
+        y, x = lax.div(place, edge), lax.rem(place, edge)
+        return y * edge + x + lax.rem(y, 2) * (edge - 1 - 2 * x)
+
+    lines = (line_at(chip), line_at(opposite(chip)))
     last = me == nx - 1
 
     barrier = pltpu.get_barrier_semaphore()
@@ -99,7 +103,8 @@
             for c in range(base, base + CHUNK):
                 total = None
                 for block, vector in terms:
-                    term = block[:, c * 128:(c + 1) * 128].astype(F32) * vector
+                    part = block[c * nz:(c + 1) * nz, :] if block.shape[-1] == 128 else block[:, c * 128:(c + 1) * 128]
+                    term = part.astype(F32) * vector
                     total = term if total is None else total + term
                 pieces.append(total)
             flat = jnp.concatenate(pieces, axis=0)
@@ -123,7 +128,10 @@
     target = lax.div(source_lane, 64) * 64 + lax.rem(source_lane, 2) * 32 + lax.div(lax.rem(source_lane, 64), 2)
     sort = jnp.where(target == lane_of((128, 128)), 1.0, 0.0).astype(BF16)
 
-    def compose(later, earlier, out):
+    def compose_rows(later, earlier, out):
+        compose(later, earlier, out, True)
+
+    def compose(later, earlier, out, by_row=False):
         lay_out(later, 0, sort)
         lay_out(earlier, 1)
         lanes = lane_of((32, 128))
@@ -133,7 +141,11 @@
             right = jnp.concatenate([
                 jnp.where(lanes < 64, b, 0.0), jnp.where(lanes < 64, turned, 0.0),
                 jnp.where(lanes < 64, 0.0, turned), jnp.where(lanes < 64, 0.0, b)], axis=0).astype(BF16)
-            out[z] = jnp.dot(square(z, 0).astype(BF16), right, preferred_element_type=F32)
+            product = jnp.dot(square(z, 0).astype(BF16), right, preferred_element_type=F32)
+            if by_row:
+                out[pl.ds(z, 32, stride=nz), :] = product
+            else:
+                out[z] = product
 
     def compose_both(later, earlier, out, flip):
         @pl.when(jnp.logical_not(flip))
@@ -193,8 +205,6 @@
 
     offsets = sorted(
         (-min(rx, edge - rx) - min(ry, edge - ry), ry, rx) for ry in range(edge) for rx in range(edge))
-    half = edge // 2
-    near = [(hops, ry, rx) for hops, ry, rx in offsets if -hops < half or (-hops == half and 1 <= rx <= half)]
 
     def beyond(ry, rx):
         return lax.rem(lax.div(chip, edge) + ry, edge) * edge + lax.rem(lax.rem(chip, edge) + rx, edge)
@@ -212,22 +222,18 @@
                 pltpu.make_async_copy(src, dst, recv).start()
 
     def to_owners(rows, index, send, recv):
-        inbox = (m_in if rows.shape[1] == 32 else b_in).at[index, slots[index]]
+        inbox = (m_in if rows.shape[1] == 32 else b_in).at[slots[index]]
         for hops, ry, rx in offsets:
             there = beyond(ry, rx)
-            if index == 0:
-                send_to(hops, 1, rows.at[there], inbox, send.at[0], recv.at[0], 2 * there + 1)
-            else:
-                send_to(hops, 0, rows.at[there], inbox, send.at[1], recv.at[1], 2 * there)
-                send_to(hops, 1, rows.at[opposite(there)], inbox, send.at[1], recv.at[1], 2 * there + 1)
+            z = line_at(there if index == 0 else opposite(there))
+            send_to(hops, 1 - index, rows.at[z], inbox, send.at[index], recv.at[index], 2 * there + 1 - index)
 
     def from_owner(boxes, index):
-        box = boxes.at[chip if index == 0 else line]
-        for hops, ry, rx in (offsets if index == 0 else near):
+        for hops, ry, rx in offsets:
             for which in range(2):
                 to = 2 * beyond(ry, rx) + which
                 step = to if index == 0 else nx - 1 - to
-                send_to(hops, which, state.at[index, step], box, e_send.at[index], e_recv.at[index], to)
+                send_to(hops, which, state.at[step], boxes.at[lines[index]], e_send, e_recv.at[index], to)
 
     def landed(ref, sem):
         pltpu.make_async_copy(ref, ref, sem).wait()
@@ -249,38 +255,38 @@
     loads[5].wait()
     mine = [widen(v_start[p], 0) for p in range(2)]
     rhs = [apply([(v_diag.at[p], widen(v_source[p], 0))]) for p in range(2)]
-
-    @pl.when(jnp.logical_not(low))
-    def _():
-        halo_dn[...] = jnp.zeros_like(halo_dn)
-
-    @pl.when(jnp.logical_not(high))
-    def _():
-        halo_up[...] = jnp.zeros_like(halo_up)
-
-    @pl.when(last)
-    def _():
-        ahead[...] = jnp.zeros_like(ahead)
-
-    @pl.when(high)
-    def _():
-        landed(halo_up, halo_recv.at[0])
-
-    @pl.when(low)
-    def _():
-        landed(halo_dn, halo_recv.at[1])
-
-    @pl.when(jnp.logical_not(last))
-    def _():
-        landed(ahead, halo_recv.at[2])
-
-    next_plane = [mine[1], widen(ahead[...], 0)]
-    fixed, drive = [], []
+    for q in range(2):
+        compose_rows(v_lower.at[1], v_side.at[q, 0], k_f.at[q])
+    fixed = []
     for p in range(2):
         below, above = shifted(mine[p])
-        fixed.append(apply([(v_side.at[0, p], widen(halo_dn[p], 0)), (v_side.at[1, p], widen(halo_up[p], 0)),
-                            (v_side.at[2, p], below), (v_side.at[3, p], above), (v_upper.at[p], next_plane[p])]))
-        drive.append(rhs[p] - fixed[p])
+        fixed.append(apply([(v_side.at[2, p], below), (v_side.at[3, p], above)]
+                           + ([(v_upper.at[0], mine[1])] if p == 0 else [])))
+    b_near = rhs[1] - fixed[1] - apply([(v_lower.at[1], rhs[0] - fixed[0])])
+
+    @pl.when(jnp.logical_not(low))
+    def _():
+        halo_dn[...] = jnp.zeros_like(halo_dn)
+
+    @pl.when(jnp.logical_not(high))
+    def _():
+        halo_up[...] = jnp.zeros_like(halo_up)
+
+    @pl.when(last)
+    def _():
+        ahead[...] = jnp.zeros_like(ahead)
+
+    @pl.when(high)
+    def _():
+        landed(halo_up, halo_recv.at[0])
+
+    @pl.when(low)
+    def _():
+        landed(halo_dn, halo_recv.at[1])
+
+    @pl.when(jnp.logical_not(last))
+    def _():
+        landed(ahead, halo_recv.at[2])
 
     def put(rows, value):
         for z in range(nz):
@@ -289,8 +295,16 @@
     def take(boxes, which):
         return jnp.concatenate([boxes[z, which] for z in range(nz)], axis=0)
 
-    put(b_f, drive[1] - apply([(v_lower.at[1], drive[0])]))
+    dn = [widen(halo_dn[p], 0) for p in range(2)]
+    up = [widen(halo_up[p], 0) for p in range(2)]
+    next_plane = widen(ahead[...], 0)
+    put(b_f, b_near - apply([(v_side.at[0, 1], dn[1]), (v_side.at[1, 1], up[1]), (v_upper.at[1], next_plane),
+                             (k_f.at[0], -dn[0]), (k_f.at[1], -up[0])]))
     to_owners(b_f, 0, b_send, b_recv)
+    for p in range(2):
+        fixed[p] = fixed[p] + apply([(v_side.at[0, p], dn[p]), (v_side.at[1, p], up[p])]
+                                    + ([(v_upper.at[1], next_plane)] if p == 1 else []))
+    drive = [rhs[p] - fixed[p] for p in range(2)]
 
     @pl.when(me >= 2)
     def _():
@@ -298,13 +312,15 @@
 
     compose_both(v_upper.at[0], v_upper.at[1], m_b, core == 0)
     to_owners(m_b, 1, m_send, m_recv)
+    for q in range(2):
+        compose_rows(v_upper.at[0], v_side.at[q, 1], k_b.at[q])
 
     def chain(boxes, index):
         if index == 0:
-            landed(m_in.at[0, pl.ds(0, nx - 1)], m_recv.at[0])
-            m_in[0, 0] = jnp.zeros((32, 128), F32)
+            landed(m_in.at[pl.ds(0, nx - 1)], m_recv.at[0])
+            m_in[0] = jnp.zeros((32, 128), F32)
         else:
-            landed(m_in.at[1], m_recv.at[1])
+            landed(m_in, m_recv.at[1])
         lanes = lane_of((32, 128))
         rows = row_of((32, 128))
         left = lanes < 64
@@ -313,30 +329,30 @@
         left_row = lane_of((1, 128)) < 64
 
         def double(j, carry):
-            a = m_in[index, 2 * j]
+            a = m_in[2 * j]
             turned = swap_halves(a)
-            m_in[index, 2 * j] = jnp.where(left, a, turned)
+            m_in[2 * j] = jnp.where(left, a, turned)
             m_odd[j] = jnp.where(left, turned, a)
             return carry
 
         lax.fori_loop(0, nx // 2, double, 0, unroll=4)
-        landed(b_in.at[index], b_recv.at[index])
+        landed(b_in, b_recv.at[index])
 
         def pair(j, x):
-            b = jnp.broadcast_to(b_in[index, 2 * j], (32, 128))
+            b = jnp.broadcast_to(b_in[2 * j], (32, 128))
             x_rows = jnp.broadcast_to(x, (32, 128))
-            even = jnp.sum(m_in[index, 2 * j] * x_rows
+            even = jnp.sum(m_in[2 * j] * x_rows
                            + jnp.where(jnp.logical_and(left, even_place), b, 0.0), axis=1, keepdims=True)
             odd = jnp.sum(m_odd[j] * x_rows
                           + jnp.where(jnp.logical_and(left, odd_place), b, 0.0), axis=1, keepdims=True)
             even, odd = jnp.broadcast_to(even, (32, 128)), jnp.broadcast_to(odd, (32, 128))
-            y = (jnp.sum(m_in[index, 2 * j + 1] * jnp.where(left, even, odd), axis=0, keepdims=True)
-                 + jnp.where(left_row, b_in[index, 2 * j + 1], 0.0))
+            y = (jnp.sum(m_in[2 * j + 1] * jnp.where(left, even, odd), axis=0, keepdims=True)
+                 + jnp.where(left_row, b_in[2 * j + 1], 0.0))
             middle = jnp.sum(jnp.where(even_place, even, jnp.where(odd_place, odd, 0.0)), axis=0, keepdims=True)
-            state[index, 2 * j, 0] = x + swap_halves(x)
-            state[index, 2 * j, 1] = middle
-            state[index, 2 * j + 1, 0] = middle
-            state[index, 2 * j + 1, 1] = y + swap_halves(y)
+            state[2 * j, 0] = x + swap_halves(x)
+            state[2 * j, 1] = middle
+            state[2 * j + 1, 0] = middle
+            state[2 * j + 1, 1] = y + swap_halves(y)
             return y
 
         lax.fori_loop(0, nx // 2, pair, jnp.zeros((1, 128), F32), unroll=True)
@@ -373,6 +389,8 @@
         below, above = shifted(f[p])
         partial.append(fixed[p] + f[p] - apply([(v_side.at[2, p], below), (v_side.at[3, p], above)]))
 
+    b_near = partial[0] - apply([(v_upper.at[0], partial[1])])
+
     @pl.when(high)
     def _():
         landed(f_up, f_recv.at[0])
@@ -381,14 +399,19 @@
     def _():
         landed(f_dn, f_recv.at[1])
 
-    g = [partial[p] - apply([(v_side.at[0, p], f_dn[p]), (v_side.at[1, p], f_up[p])]) for p in range(2)]
-    put(b_b, g[0] - apply([(v_upper.at[0], g[1])]))
+    dn, up = [f_dn[p] for p in range(2)], [f_up[p] for p in range(2)]
+    put(b_b, b_near - apply([(v_side.at[0, 0], dn[0]), (v_side.at[1, 0], up[0]), (k_b.at[0], -dn[1]), (k_b.at[1], -up[1])]))
     to_owners(b_b, 1, b_send, b_recv)
-    chain(e_b, 1)
+    drive_1 = partial[1] - apply([(v_side.at[0, 1], dn[1]), (v_side.at[1, 1], up[1])])
+
+    @pl.when(core == 0)
+    def _():
+        chain(e_b, 1)
+
 
     landed(e_b, e_recv.at[1])
     result_out[0] = narrow(take(e_b, 1))
-    result_out[1] = narrow(g[1] - apply([(v_upper.at[1], take(e_b, 0))]))
+    result_out[1] = narrow(drive_1 - apply([(v_upper.at[1], take(e_b, 0))]))
 
     @pl.when(low)
     def _():
@@ -404,23 +427,16 @@
     def _():
         landed(ahead, halo_send.at[2])
 
-    @pl.when(core == 1)
-    def _():
-        landed(m_f.at[pl.ds(0, nz - 1)], m_send.at[0])
-        landed(b_f.at[pl.ds(0, nz - 1)], b_send.at[0])
-        landed(state.at[0, pl.ds(0, nx - 1)], e_send.at[0])
-
-    @pl.when(core == 0)
-    def _():
-        landed(b_f, b_send.at[0])
-
-    @pl.when(jnp.logical_and(core == 0, before))
-    def _():
-        landed(m_f, m_send.at[0])
-
-    landed(m_in.at[1, pl.ds(0, nx - 1)], m_send.at[1])
-    landed(b_in.at[1, pl.ds(0, nx - 1)], b_send.at[1])
-    landed(state.at[1, pl.ds(0, nz - 1)], e_send.at[1])
+    for index, rows, sem, sends in ((0, m_f, m_send, before), (0, b_f, b_send, True), (1, m_b, m_send, True), (1, b_b, b_send, True)):
+        @pl.when(jnp.logical_and(core == 1 - index, sends))
+        def _():
+            landed(rows.at[pl.ds(0, nz - 1)], sem.at[index])
+
+        @pl.when(jnp.logical_and(core == index, sends))
+        def _():
+            landed(rows, sem.at[index])
+
+    landed(state.at[pl.ds(0, nx - 1)], e_send)
 
 
 def hand_out(forward_in, result_in, forward_out, result_out):
@@ -450,12 +466,13 @@
                 pltpu.VMEM((4, 2, nz, width), BF16),
                 pltpu.VMEM((2, half, 128), F32), pltpu.VMEM((2, half, 128), F32), pltpu.VMEM((half, 128), F32),
                 pltpu.VMEM((nz + 16, 128), F32), pltpu.VMEM((nz, 128), F32), pltpu.VMEM((2 * 32 * nz, 128), F32),
-                pltpu.VMEM((nz, 32, 128), F32), pltpu.VMEM((nz, 32, 128), F32), pltpu.VMEM((2, nx, 32, 128), F32),
-                pltpu.VMEM((nz, 1, 128), F32), pltpu.VMEM((nz, 1, 128), F32), pltpu.VMEM((2, nx, 1, 128), F32),
-                pltpu.VMEM((2, nx, 2, 1, 128), F32),
+                pltpu.VMEM((nz, 32, 128), F32), pltpu.VMEM((nz, 32, 128), F32), pltpu.VMEM((nx, 32, 128), F32),
+                pltpu.VMEM((nz, 1, 128), F32), pltpu.VMEM((nz, 1, 128), F32), pltpu.VMEM((nx, 1, 128), F32),
+                pltpu.VMEM((nx, 2, 1, 128), F32),
                 pltpu.VMEM((nz, 2, 1, 128), F32), pltpu.VMEM((nz, 2, 1, 128), F32), pltpu.VMEM((nx // 2, 32, 128), F32),
+                pltpu.VMEM((2, 32 * nz, 128), F32), pltpu.VMEM((2, 32 * nz, 128), F32),
                 pltpu.VMEM((2, nz, 128), F32), pltpu.VMEM((2, nz, 128), F32), pltpu.VMEM((2, nz, 128), F32),
-                dma((6,)), dma((3,)), dma((3,)), dma((2,)), dma((2,)), dma((2,)), dma((2,)), dma((2,)), dma((2,)),
+                dma((6,)), dma((3,)), dma((3,)), dma((2,)), dma((2,)), dma((2,)), dma((2,)), dma, dma((2,)),
                 dma((2,)), dma((2,)), pltpu.SemaphoreType.REGULAR,
             ],
             compiler_params=pltpu.CompilerParams(collective_id=0, has_side_effects=True),

time: 39.2 us -> 38.6 us (0.985)
  Pallas kernels: 38.5 us -> 37.8 us
    pallas_call x1, Pallas kernels: 37.9 us -> 37.2 us  [local(): pl.pallas_call(functools.partial(kernel, nx, ny, nz), out_shape=(pltpu.VM...]
where the time goes in v4:
time: 38.6 us; the launch traced here: 38.4 us
  Pallas kernels  37.8 us (98%)
  between operations  0.64 us (2%)
    pallas_call x1, Pallas kernels, local(): pl.pallas_call(functools.partial(kernel, nx, ny, nz), out_shape=(pltpu.VM...  37.2 us

profile of v4, /device:TPU:193, one launch (start us, length us, event | category | flops | bytes accessed | tf_op | source)
XLA Modules:
  0.0 38.4 jit_solution(13476514188600981651)
XLA Ops:
  0.6 37.2 %shard_map.77 = (f32[2,8,128]{2,1,0:T(8,128)S(1)}, f32[2,8,128]{2,1,0:T(8,128)S(1)}) custom-call(f32[2,8,128]{2,1,0:T(8,128)} %bitcast.12, f32[2,8,128]{2,1,0:T(8,128)} %bitcast.13, bf16[2,16,4096]{2,1,0:T(8,128)(2,1)} %bitcast.9, bf16[2,16,4096]{2,1,0:T(8,128)(2,1)} %bitcast.10, bf16[2,16,4096]{2,1,0:T(8,128)(2,1)} %bitcast.11, bf16[4,2,16,4096]{3,2,1,0:T(8,128)(2,1)} %bitcast.8), custom_call_target="tpu_custom_call" | custom-call | tf_op jit(solution)/shard_map/pallas_call | solution.py:458
  37.8 0.6 %shard_map.78 = (f32[2,8,128]{2,1,0:T(8,128)}, f32[2,8,128]{2,1,0:T(8,128)}) custom-call(f32[2,8,128]{2,1,0:T(8,128)S(1)} %get-tuple-element.6.forward_in, f32[2,8,128]{2,1,0:T(8,128)S(1)} %get-tuple-element.7.result_in), custom_call_target="tpu_custom_call" | custom-call | tf_op jit(solution)/shard_map/pallas_call | solution.py:483

commit v5 on v4

--- a/solution.py
+++ b/solution.py
@@ -180,11 +180,6 @@
 
     pl.semaphore_wait(barrier, nx - 2 + low.astype(jnp.int32) + high.astype(jnp.int32) + (me == 0).astype(jnp.int32))
 
-    @pl.when(me == 0)
-    def _():
-        greet(hello)
-        loads[1].wait()
-
     loads[0].wait()
 
     def copy(src, dst, send, recv, where):
@@ -198,6 +193,11 @@
     @pl.when(high)
     def _():
         copy(v_start, halo_dn, halo_send.at[1], halo_recv.at[1], (me, my + 1)).start()
+
+    @pl.when(me == 0)
+    def _():
+        greet(hello)
+        loads[1].wait()
 
     @pl.when(me >= 2)
     def _():
@@ -439,9 +439,13 @@
     landed(state.at[pl.ds(0, nx - 1)], e_send)
 
 
-def hand_out(forward_in, result_in, forward_out, result_out):
-    forward_out[...] = forward_in[...]
-    result_out[...] = result_in[...]
+def hand_out(forward_in, result_in, forward_out, result_out, sem):
+    copies = [pltpu.make_async_copy(forward_in, forward_out, sem.at[0]),
+              pltpu.make_async_copy(result_in, result_out, sem.at[1])]
+    for one in copies:
+        one.start()
+    for one in copies:
+        one.wait()
 
 
 def solution(mesh):
@@ -481,7 +485,8 @@
         forward = pltpu.with_memory_space_constraint(forward, pltpu.VMEM)
         result = pltpu.with_memory_space_constraint(result, pltpu.VMEM)
         forward, result = pl.pallas_call(
-            hand_out, out_shape=(out, out), in_specs=[vmem, vmem], out_specs=(vmem, vmem))(forward, result)
+            hand_out, out_shape=(out, out), in_specs=[vmem, vmem], out_specs=(any_space, any_space),
+            scratch_shapes=[dma((2,))])(forward, result)
         return forward.reshape(start.shape), result.reshape(start.shape)
 
     return jax.shard_map(

time: 38.6 us -> 38.5 us (level)
  no operation moved by 1% of the time
where the time goes in v5:
time: 38.5 us; the launch traced here: 38.4 us
  Pallas kernels  37.7 us (98%)
  between operations  0.64 us (2%)
    pallas_call x1, Pallas kernels, local(): pl.pallas_call(functools.partial(kernel, nx, ny, nz), out_shape=(pltpu.VM...  37.1 us

profile of v5, /device:TPU:193, one launch (start us, length us, event | category | flops | bytes accessed | tf_op | source)
XLA Modules:
  0.0 38.4 jit_solution(13142591644041271891)
XLA Ops:
  0.6 37.1 %shard_map.77 = (f32[2,8,128]{2,1,0:T(8,128)S(1)}, f32[2,8,128]{2,1,0:T(8,128)S(1)}) custom-call(f32[2,8,128]{2,1,0:T(8,128)} %bitcast.12, f32[2,8,128]{2,1,0:T(8,128)} %bitcast.13, bf16[2,16,4096]{2,1,0:T(8,128)(2,1)} %bitcast.9, bf16[2,16,4096]{2,1,0:T(8,128)(2,1)} %bitcast.10, bf16[2,16,4096]{2,1,0:T(8,128)(2,1)} %bitcast.11, bf16[4,2,16,4096]{3,2,1,0:T(8,128)(2,1)} %bitcast.8), custom_call_target="tpu_custom_call" | custom-call | tf_op jit(solution)/shard_map/pallas_call | solution.py:462
  37.7 0.6 %shard_map.78 = (f32[2,8,128]{2,1,0:T(8,128)}, f32[2,8,128]{2,1,0:T(8,128)}) custom-call(f32[2,8,128]{2,1,0:T(8,128)S(1)} %get-tuple-element.6.forward_in, f32[2,8,128]{2,1,0:T(8,128)S(1)} %get-tuple-element.7.result_in), custom_call_target="tpu_custom_call" | custom-call | tf_op jit(solution)/shard_map/pallas_call | solution.py:487
